TPU v7x, 128 devices: a whole 4x4x4 slice. The times are simulated.
128 devices in a mesh: gr: 16 (over x, y_hi, core), gc: 8 (over z, y_lo).
Axes of the slice: x: 4, y: 4 (y_hi: 2, y_lo: 2; y = y_hi * 2 + y_lo), z: 4, core: 2. Of those that a mesh axis runs over, the one named last changes fastest.
Arguments:
- returns: bfloat16 [16384, 8192], P(('gr', 'gc')), may hold values from -6 to 6
- start_seed: int32 [8192, 64], replicated, may hold values from -1000 to 999
Outputs:
- loadings: float32 [8192, 64], P('gr')
- strengths: float32 [3, 64], replicated
All inputs are finite; a program needn't handle non-finite values.
Results may differ from a plain program's by a relative error of at most 0.0003.
Values may be sent and summed in bfloat16 or wider, within the bound.
A program may use at most 128 MiB of HBM per device.

v0:
```python
import math

import jax
import jax.numpy as jnp
from jax import lax
from jax.sharding import PartitionSpec as P

ITERS = 3


def orthonormal(applied, inner_gram):
    factor = jnp.linalg.cholesky(inner_gram)
    solved = lax.linalg.triangular_solve(
        factor, applied, left_side=False, lower=True, transpose_a=True
    )
    return (solved, jnp.diagonal(factor))


def local_gram(applied):
    return jnp.dot(applied.T, applied, precision=lax.Precision.HIGHEST)


def local(returns, start_seed):
    asset_count = returns.shape[1]
    day_count = returns.shape[0] * lax.axis_size("gr") * lax.axis_size("gc")
    row_span = asset_count // lax.axis_size("gr")
    row_place = lax.axis_index("gr")
    start_vectors = start_seed.astype(jnp.float32) / 1000.0
    diagonals = []
    returns_wide = returns.astype(jnp.float32)
    vectors = start_vectors
    for sweep in range(ITERS):
        projected = jnp.dot(returns_wide, vectors, precision=lax.Precision.HIGHEST)
        partial_apply = lax.dot_general(
            returns_wide, projected, (((0,), (0,)), ((), ())), precision=lax.Precision.HIGHEST
        )
        applied = lax.psum(partial_apply, ("gr", "gc")) / day_count
        vectors, diag_part = orthonormal(applied, local_gram(applied))
        diagonals.append(diag_part)
    vectors = lax.dynamic_slice_in_dim(vectors, row_place * row_span, row_span, 0)
    return (vectors * math.sqrt(asset_count), jnp.stack(diagonals, axis=0))


def solution(mesh):
    placed = (P(("gr", "gc"), None), P())
    return jax.shard_map(
        local, mesh=mesh, in_specs=placed, out_specs=(P("gr", None), P()), check_vma=False
    )
```

profile of v0, /device:TPU:1, one launch (start us, length us, event | category | flops | bytes accessed | tf_op | source)
XLA Modules:
  0.0 545.8 jit_solution(4861265204526144004)
XLA Ops:
  7.2 0.0 copy-start
  7.2 0.0 all-reduce.4.cloned.1.call-start
  7.2 1.5 copy-done
  8.8 3.9 fusion
  12.7 2.3 convolution_bitcast_fusion.5
  15.0 0.0 all-reduce.4.cloned.1.call-update
  15.0 0.0 all-reduce.6.cloned.1.call-start
  15.0 154.3 %all-reduce.4.cloned.1.call-done = f32[8192,64]{0,1:T(8,128)} async-done(((f32[8192,64]{0,1:T(8,128)}), f32[8192,64]{0,1:T(8,128)}) %all-reduce.4.cloned.1.call-update) | async-done | bytes 2097168 | tf_op jit(solution)/shard_map/psum | solution.py:37
  169.4 4.1 fusion.10
  173.5 0.1 copy.7
  173.6 5.8 %cholesky.59 = f32[64,64]{1,0:T(8,128)S(1)} custom-call(f32[64,64]{1,0:T(8,128)S(1)} %fusion.24), custom_call_target="Cholesky" | custom-call | tf_op jit(solution)/shard_map/jit(cholesky)/cholesky | solution.py:12
  179.5 0.6 compare_reduce_fusion.2
  180.1 0.7 fusion.31
  180.8 4.9 custom-call.13
  185.7 3.5 convolution_bitcast_fusion.4
  189.2 2.3 fusion.46
  191.5 2.3 convolution_bitcast_fusion.3
  193.7 0.0 all-reduce.6.cloned.1.call-update
  193.8 0.2 all-reduce.8.cloned.1.call-start
  194.0 149.3 %all-reduce.6.cloned.1.call-done = f32[8192,64]{0,1:T(8,128)} async-done(((f32[8192,64]{0,1:T(8,128)}), f32[8192,64]{0,1:T(8,128)}) %all-reduce.6.cloned.1.call-update) | async-done | bytes 2097168 | tf_op jit(solution)/shard_map/psum | solution.py:37
  343.3 4.1 fusion.7
  347.4 0.1 copy.8
  347.5 5.8 %cholesky.70 = f32[64,64]{1,0:T(8,128)S(1)} custom-call(f32[64,64]{1,0:T(8,128)S(1)} %fusion.22), custom_call_target="Cholesky" | custom-call | tf_op jit(solution)/shard_map/jit(cholesky)/cholesky | solution.py:12
  353.4 0.6 compare_reduce_fusion.1
  354.0 0.7 fusion.30
  354.7 4.9 custom-call.14
  359.6 3.5 convolution_bitcast_fusion.2
  363.1 2.3 fusion.47
  365.4 2.3 convolution_bitcast_fusion.1
  367.6 0.0 all-reduce.8.cloned.1.call-update
  367.7 0.8 gather_fusion
  368.5 0.8 gather_fusion.1
  369.3 147.9 %all-reduce.8.cloned.1.call-done = f32[8192,64]{0,1:T(8,128)} async-done(((f32[8192,64]{0,1:T(8,128)}), f32[8192,64]{0,1:T(8,128)}) %all-reduce.8.cloned.1.call-update) | async-done | bytes 2097168 | tf_op jit(solution)/shard_map/psum | solution.py:37
  517.2 4.1 fusion.4
  521.4 0.1 copy.9
  521.4 5.8 %cholesky.81 = f32[64,64]{1,0:T(8,128)S(1)} custom-call(f32[64,64]{1,0:T(8,128)S(1)} %fusion.20), custom_call_target="Cholesky" | custom-call | tf_op jit(solution)/shard_map/jit(cholesky)/cholesky | solution.py:12
  527.3 0.6 compare_reduce_fusion
  528.0 0.7 select_bitcast_fusion
  528.6 5.0 custom-call.15
  533.7 0.8 gather_fusion.2
  534.5 3.5 convolution_bitcast_fusion
  538.0 0.7 dynamic-slice_multiply_fusion
  538.6 0.6 pad_maximum_fusion
  (7 shorter events, 0.1 us)
Async XLA Ops:
  7.2 1.6 copy-start
  7.2 162.2 %all-reduce.4.cloned.1.call-start = ((), (), s32[]{:S(2)}) async-start(), calls=%async_computation | async-start | bytes 4194304 | tf_op jit(solution)/shard_map/psum | solution.py:37
  15.0 328.3 %all-reduce.6.cloned.1.call-start = ((), (), s32[]{:S(2)}) async-start(), calls=%async_computation.1 | async-start | bytes 4194304 | tf_op jit(solution)/shard_map/psum | solution.py:37
  193.8 323.4 %all-reduce.8.cloned.1.call-start = ((), (), s32[]{:S(2)}) async-start(), calls=%async_computation.2 | async-start | bytes 4194304 | tf_op jit(solution)/shard_map/psum | solution.py:37
Sparse Core Ops, SparseCore 0:
  15.1 154.2 all-reduce.3
  193.9 149.3 all-reduce.5
  367.8 149.3 all-reduce.7
where the time goes:
time: 546 us
  waiting for transfers between devices  452 us (83%)
  matrix products  38.2 us (7%)
  other arithmetic  37.7 us (7%)
  between operations  13.9 us (3%)
    psum x3, waiting for transfers between devices, local(): applied = lax.psum(partial_apply, ('gr', 'gc')) / day_count  451 us
    another operation x9, other arithmetic, orthonormal(): factor = jnp.linalg.cholesky(inner_gram)  19.6 us
    another operation x6, other arithmetic, orthonormal(): lax.linalg.triangular_solve(factor, applied, left_side=False, lower=True,...  16.8 us
    dot_general x3, matrix products, local_gram(): return jnp.dot(applied.T, applied, precision=lax.Precision.HIGHEST)  12.4 us
  transfers between devices with their start and end apart: 3, of which 3 were waited for; matrix products, arithmetic and copies ran while one was open for 0% of the time, Pallas kernels for 0%

commit v1 on v0

v1 whole, which is shorter than its diff:
```python
import functools
import math

import jax
import jax.numpy as jnp
from jax import lax
from jax.experimental import pallas as pl
from jax.experimental.pallas import tpu as pltpu
from jax.sharding import PartitionSpec as P

ITERS = 3
MESH = pl.DeviceIdType.MESH
F32 = jnp.float32
BF16 = jnp.bfloat16
NT = (((1,), (1,)), ((), ()))


def split3(a):
    hi = a.astype(BF16)
    rest = a - hi.astype(F32)
    mid = rest.astype(BF16)
    low = (rest - mid.astype(F32)).astype(BF16)
    return jnp.concatenate([hi, mid, low], axis=0)


def fold3(a):
    return a[0:64] + (a[64:128] + a[128:192])


def factor(gram):
    lane = lax.broadcasted_iota(jnp.int32, (8, 128), 1)
    sub = lax.broadcasted_iota(jnp.int32, (8, 128), 0)
    wide = jnp.concatenate([jnp.zeros((64, 64), F32), gram], axis=1)
    rows = [
        jnp.where(lane == sub + 8 * g, 1.0, wide[8 * g : 8 * g + 8]) for g in range(8)
    ]
    for j in range(64):
        g0, r = divmod(j, 8)
        pivot = jnp.broadcast_to(rows[g0][r : r + 1, :], (8, 128))
        d = jnp.broadcast_to(pivot[:, 64 + j : 65 + j], (8, 128))
        scaled = pivot / d
        for g in range(g0, 8):
            col = jnp.broadcast_to(rows[g][:, 64 + j : 65 + j], (8, 128))
            if g == g0:
                col = jnp.where(sub > r, col, 0.0)
            rows[g] = rows[g] - col * scaled
    inverse = []
    diag = jnp.zeros((8, 128), F32)
    for g in range(8):
        mask = lane == sub + (8 * g + 64)
        d = jnp.sum(jnp.where(mask, rows[g], 0.0), axis=1, keepdims=True)
        root = jnp.broadcast_to(jnp.sqrt(d), (8, 128))
        inverse.append(rows[g] / root)
        diag = diag + jnp.where(mask, root, 0.0)
    inverse = jnp.concatenate(inverse, axis=0)[:, 0:64]
    return inverse, jnp.sum(diag, axis=0, keepdims=True)[:, 64:128]


def kernel(
    days, r_ref, seed_ref, load_ref, str_ref,
    rb, seeds, pbuf, pc, abuf, r1, bbuf, r2, ybuf, ag, gbuf, fin, gx, gz,
    send, recv,
):
    gr = lax.axis_index("gr")
    gc = lax.axis_index("gc")
    core = gr % 2
    x = gr // 4
    y = (gr // 2) % 2 * 2 + gc % 2
    z = gc // 2

    def dev(x, y, z, core):
        return ((x * 2 + y // 2) * 2 + core, z * 2 + y % 2)

    partner = dev(x, y, z, 1 - core)
    xp = [dev((x + o) % 4, y, z, core) for o in (1, 2, 3)]
    yp = [dev(x, (y + o) % 4, z, core) for o in (1, 2, 3)]
    zp = [dev(x, y, (z + o) % 4, core) for o in (1, 2, 3)]

    barrier = pltpu.get_barrier_semaphore()
    everyone = [partner] + xp + yp + zp
    for device in everyone:
        pl.semaphore_signal(barrier, inc=1, device_id=device, device_id_type=MESH)
    pl.semaphore_wait(barrier, len(everyone))

    count = [0]
    pending = []

    def push(src, dst, device):
        k = count[0]
        count[0] += 1
        copy = pltpu.make_async_remote_copy(
            src_ref=src, dst_ref=dst, send_sem=send.at[k], recv_sem=recv.at[k],
            device_id=device, device_id_type=MESH,
        )
        copy.start()
        pending.append(copy)
        return copy

    mine = pl.ds(pl.multiple_of(core * 128, 128), 128)
    swaps = []
    for s in range(8):
        cols = pl.ds(pl.multiple_of((2 * s + 1 - core) * 512, 512), 512)
        swaps.append(push(r_ref.at[:, cols], rb.at[mine, pl.ds(s * 512, 512)], partner))
    for s in range(8):
        cols = pl.ds(pl.multiple_of((2 * s + core) * 512, 512), 512)
        rb[mine, pl.ds(s * 512, 512)] = r_ref[:, cols]

    for c in range(8):
        part = seed_ref[:, c * 1024 : (c + 1) * 1024].astype(F32)
        hi = part.astype(BF16)
        low = (part - hi.astype(F32)).astype(BF16)
        seeds[0:64, c * 1024 : (c + 1) * 1024] = hi
        seeds[64:128, c * 1024 : (c + 1) * 1024] = low
    first = lax.dot_general(seeds[...], r_ref[...], NT, preferred_element_type=F32)
    pbuf[0, core, :, 0:128] = (first[0:64] + first[64:128]) / 1000.0
    copy = push(pbuf.at[0, core, :, 0:128], pbuf.at[0, core, :, 0:128], partner)
    copy.wait_recv()
    for swap in swaps:
        swap.wait_recv()
    projected = jnp.concatenate([pbuf[0, 0, :, 0:128], pbuf[0, 1, :, 0:128]], axis=1)

    peers = ((xp, zp), (zp, xp))
    place = ((x, z), (z, x))
    inverse = None
    for it in range(ITERS):
        p3 = split3(projected * (1.0 / days))
        for s in range(8):
            out = fold3(jnp.dot(p3, rb[:, s * 512 : (s + 1) * 512], preferred_element_type=F32))
            for j in range(4):
                h, xq = s % 2, s // 2
                block = out[:, j * 128 : (j + 1) * 128]
                if h == 0:
                    abuf[it, 0, xq, j] = block
                else:
                    abuf[it, 1, j, xq] = block
        copies = []
        for h in range(2):
            for o in (1, 0, 2):
                to = (place[h][0] + o + 1) % 4
                copies.append(push(abuf.at[it, h, to], r1.at[it, h, o], peers[h][0][o]))
        if it > 0:
            square = fold_gram(lax.dot_general(pc[...], pc[...], NT, preferred_element_type=F32))
            gbuf[it - 1, core, :, 0:64] = square
            copy = push(gbuf.at[it - 1, core], gbuf.at[it - 1, core], partner)
            copy.wait_recv()
            inverse, diag = factor(gbuf[it - 1, 0, :, 0:64] + gbuf[it - 1, 1, :, 0:64])
            str_ref[it - 1 : it, :] = diag
        for copy in copies:
            copy.wait_recv()
        copies = []
        for h in range(2):
            bbuf[it, h] = (abuf[it, h, place[h][0]] + r1[it, h, 0]) + (r1[it, h, 1] + r1[it, h, 2])
        for h in range(2):
            for o in (1, 0, 2):
                to = (place[h][1] + o + 1) % 4
                copies.append(push(bbuf.at[it, h, to], r2.at[it, h, o], peers[h][1][o]))
        for copy in copies:
            copy.wait_recv()
        for h in range(2):
            ybuf[it, y, h] = (bbuf[it, h, place[h][1]] + r2[it, h, 0]) + (r2[it, h, 1] + r2[it, h, 2])
        copies = [push(ybuf.at[it, y], ybuf.at[it, y], yp[o]) for o in (1, 0, 2)]
        for copy in copies:
            copy.wait_recv()
        done = [(ybuf[it, 0, h] + ybuf[it, 1, h]) + (ybuf[it, 2, h] + ybuf[it, 3, h]) for h in range(2)]
        if it > 0:
            both = jnp.dot(inverse, jnp.concatenate(done, axis=1), precision=lax.Precision.HIGHEST, preferred_element_type=F32)
            done = [both[:, 0:128], both[:, 128:256]]
        if it == ITERS - 1:
            break
        copies = []
        for h in range(2):
            ag[it, h, place[h][0], place[h][1]] = done[h]
        for h in range(2):
            block = ag.at[it, h, place[h][0], place[h][1]]
            for o in (1, 0, 2):
                copies.append(push(block, block, peers[h][1][o]))
        for copy in copies:
            copy.wait_recv()
        copies = []
        for h in range(2):
            block = ag.at[it, h, place[h][0]]
            for o in (1, 0, 2):
                copies.append(push(block, block, peers[h][0][o]))
        for copy in copies:
            copy.wait_recv()
        for s in range(8):
            for j in range(4):
                h, xq = s % 2, s // 2
                block = ag[it, 0, xq, j] if h == 0 else ag[it, 1, j, xq]
                pc[:, (4 * s + j) * 128 : (4 * s + j + 1) * 128] = split3(block)
        pbuf[it + 1, core] = fold3(lax.dot_general(pc[...], rb[...], NT, preferred_element_type=F32))
        copy = push(pbuf.at[it + 1, core], pbuf.at[it + 1, core], partner)
        copy.wait_recv()
        projected = pbuf[it + 1, 0] + pbuf[it + 1, 1]

    fin[z] = jnp.where(y < 2, done[0], done[1])
    last = [push(fin.at[z], fin.at[z], zp[o]) for o in (1, 0, 2)]
    whole = jnp.concatenate(done, axis=1)
    wide = split3(whole)
    gx[x, :, 0:64] = fold_gram(lax.dot_general(wide, wide, NT, preferred_element_type=F32))
    copies = [push(gx.at[x], gx.at[x], xp[o]) for o in (1, 0, 2)]
    for copy in copies:
        copy.wait_recv()
    gz[z] = (gx[0] + gx[1]) + (gx[2] + gx[3])
    copies = [push(gz.at[z], gz.at[z], zp[o]) for o in (1, 0, 2)]
    for copy in copies:
        copy.wait_recv()
    gbuf[2, core] = (gz[0] + gz[1]) + (gz[2] + gz[3])
    copy = push(gbuf.at[2, core], gbuf.at[2, core], partner)
    copy.wait_recv()
    inverse, diag = factor(gbuf[2, 0, :, 0:64] + gbuf[2, 1, :, 0:64])
    str_ref[2:3, :] = diag
    for copy in last:
        copy.wait_recv()
    slab = jnp.concatenate([fin[k] for k in range(4)], axis=1)
    out = jnp.dot(inverse, slab, precision=lax.Precision.HIGHEST, preferred_element_type=F32)
    load_ref[...] = out * math.sqrt(8192)
    for copy in pending:
        copy.wait_send()


def fold_gram(a):
    hh, hm, hl = a[0:64, 0:64], a[0:64, 64:128], a[0:64, 128:192]
    mh, mm, lh = a[64:128, 0:64], a[64:128, 64:128], a[128:192, 0:64]
    return hh + ((hm + mh) + (mm + (hl + lh)))


SEMS = 128


def local(days, returns, start_seed):
    seed = start_seed.T
    vm = pltpu.VMEM
    out = pl.pallas_call(
        functools.partial(kernel, days),
        out_shape=(
            jax.ShapeDtypeStruct((64, 512), F32),
            jax.ShapeDtypeStruct((3, 64), F32),
        ),
        in_specs=[pl.BlockSpec(memory_space=pltpu.VMEM)] * 2,
        out_specs=[pl.BlockSpec(memory_space=pltpu.VMEM)] * 2,
        scratch_shapes=[
            vm((256, 4096), BF16),
            vm((128, 8192), BF16),
            vm((3, 2, 64, 256), F32),
            vm((192, 4096), BF16),
            vm((3, 2, 4, 4, 64, 128), F32),
            vm((3, 2, 3, 4, 64, 128), F32),
            vm((3, 2, 4, 64, 128), F32),
            vm((3, 2, 3, 64, 128), F32),
            vm((3, 4, 2, 64, 128), F32),
            vm((2, 2, 4, 4, 64, 128), F32),
            vm((3, 2, 64, 128), F32),
            vm((4, 64, 128), F32),
            vm((4, 64, 128), F32),
            vm((4, 64, 128), F32),
            pltpu.SemaphoreType.DMA((SEMS,)),
            pltpu.SemaphoreType.DMA((SEMS,)),
        ],
        compiler_params=pltpu.CompilerParams(
            collective_id=0, has_side_effects=True, vmem_limit_bytes=40 * 2**20
        ),
        name="power",
    )(returns, seed)
    return out[0].T, out[1]


def solution(mesh):
    placed = (P(("gr", "gc"), None), P())
    return jax.shard_map(
        functools.partial(local, 16384), mesh=mesh, in_specs=placed,
        out_specs=(P("gr", None), P()), check_vma=False,
    )
```

time: 546 us -> 119 us (0.22)
  waiting for transfers between devices: 452 us -> 0 us
  Pallas kernels: 0 us -> 114 us
  matrix products: 38.2 us -> 0 us
  other arithmetic: 37.7 us -> 0 us
  between operations: 13.9 us -> 0.65 us
    psum x3 -> x0, waiting for transfers between devices: 451 us -> none  [local(): applied = lax.psum(partial_apply, ('gr', 'gc')) / day_count]
    pallas_call x0 -> x1, Pallas kernels: none -> 114 us  [local(): pl.pallas_call(functools.partial(kernel, days), out_shape=(jax.ShapeDtype...]
    another operation x16 -> x0, other arithmetic: 36.9 us -> none  [the longest x9 19.6 us: orthonormal(): factor = jnp.linalg.cholesky(inner_gram)]
    dot_general x9 -> x0, matrix products: 27.8 us -> none  [the longest x3 12.4 us: local_gram(): return jnp.dot(applied.T, applied, precision=lax.Precision.HIGHEST)]
    another operation x3 -> x0, matrix products: 10.4 us -> none  [orthonormal(): lax.linalg.triangular_solve(factor, applied, left_side=False, lower=True,...]
  transfers between devices with their start and end apart: 3 -> 0, of which waited for: 3 -> 0; matrix products, arithmetic and copies ran while one was open for 0% -> 0% of each run, Pallas kernels for 0% -> 0%
where the time goes in v1:
time: 119 us
  Pallas kernels  114 us (96%)
  local copies, waits for them, and re-layouts  4.41 us (4%)
    pallas_call x1, Pallas kernels, local(): pl.pallas_call(functools.partial(kernel, days), out_shape=(jax.ShapeDtype...  114 us
    unnamed x6, local copies, waits for them, and re-layouts  4.41 us

profile of v1, /device:TPU:1, one launch (start us, length us, event | category | flops | bytes accessed | tf_op | source)
XLA Modules:
  0.0 118.9 jit_solution(2926166836532111409)
XLA Ops:
  0.6 0.0 copy-start
  0.6 1.6 %copy-done = bf16[128,8192]{1,0:T(8,128)(2,1)S(1)} copy-done((bf16[128,8192]{1,0:T(8,128)(2,1)S(1)}, bf16[128,8192]{1,0:T(8,128)(2,1)}, u32[]{:S(2)}) %copy-start) | copy-done | bytes 2097176
  2.2 0.0 copy-start.1
  2.2 1.6 %copy-done.1 = s32[8192,64]{0,1:T(8,128)S(1)} copy-done((s32[8192,64]{0,1:T(8,128)S(1)}, s32[8192,64]{0,1:T(8,128)}, u32[]{:S(2)}) %copy-start.1) | copy-done | bytes 2097176
  3.8 113.8 %power.1 = (f32[64,512]{1,0:T(8,128)S(1)}, f32[3,64]{1,0:T(4,128)S(1)}) custom-call(bf16[128,8192]{1,0:T(8,128)(2,1)S(1)} %copy-done, s32[64,8192]{1,0:T(8,128)S(1)} %bitcast.2), custom_call_target="tpu_custom_call" | custom-call | tf_op jit(solution)/shard_map/power/pallas_call | solution.py:234
  117.6 0.7 copy.6
  118.3 0.6 copy.7
Async XLA Ops:
  0.6 1.6 %copy-start = (bf16[128,8192]{1,0:T(8,128)(2,1)S(1)}, bf16[128,8192]{1,0:T(8,128)(2,1)}, u32[]{:S(2)}) copy-start(bf16[128,8192]{1,0:T(8,128)(2,1)} %r_ref.1) | copy-start | bytes 6291460
  2.2 1.6 %copy-start.1 = (s32[8192,64]{0,1:T(8,128)S(1)}, s32[8192,64]{0,1:T(8,128)}, u32[]{:S(2)}) copy-start(s32[8192,64]{0,1:T(8,128)} %param.3) | copy-start | bytes 6291460

commit v2 on v0

v2 whole, which is shorter than its diff:
```python
import functools
import math

import jax
import jax.numpy as jnp
from jax import lax
from jax.experimental import pallas as pl
from jax.experimental.pallas import tpu as pltpu
from jax.sharding import PartitionSpec as P

ITERS = 3
MESH = pl.DeviceIdType.MESH
F32 = jnp.float32
BF16 = jnp.bfloat16
NN = (((1,), (0,)), ((), ()))
NT = (((1,), (1,)), ((), ()))


def dot(a, b, dims=NN):
    return lax.dot_general(a, b, dims, preferred_element_type=F32)


def exact(a, b, dims=NN):
    return lax.dot_general(a, b, dims, precision=lax.Precision.HIGHEST, preferred_element_type=F32)


def split3(a):
    hi = a.astype(BF16)
    rest = a - hi.astype(F32)
    mid = rest.astype(BF16)
    low = (rest - mid.astype(F32)).astype(BF16)
    return jnp.concatenate([hi, mid, low], axis=0)


def fold(a):
    return a[0:32] + (a[32:64] + a[64:96])


def fold2(a):
    hh, hm, hl = a[0:32, 0:32], a[0:32, 32:64], a[0:32, 64:96]
    mh, mm, lh = a[32:64, 0:32], a[32:64, 32:64], a[64:96, 0:32]
    return hh + ((hm + mh) + (mm + (hl + lh)))


def factor32(gram):
    lane = lax.broadcasted_iota(jnp.int32, (8, 128), 1)
    sub = lax.broadcasted_iota(jnp.int32, (8, 128), 0)
    bc = lambda a: jnp.broadcast_to(a, (8, 128))
    zero = jnp.zeros((32, 32), F32)
    wide = jnp.concatenate([zero, zero, gram, zero], axis=1)
    rows = [jnp.where(lane == sub + 8 * g, 1.0, wide[8 * g : 8 * g + 8]) for g in range(4)]
    for j in range(0, 32, 4):
        g0, r = divmod(j, 8)
        cols = [[bc(rows[g][:, 64 + j + k : 65 + j + k]) for g in range(g0, 4)] for k in range(4)]
        p = [bc(rows[g0][r + k : r + k + 1, :]) for k in range(4)]
        a = [[bc(cols[k][0][r + i : r + i + 1, :]) for k in range(i + 1)] for i in range(4)]
        idet = 1.0 / (a[0][0] * a[1][1] - a[1][0] * a[1][0])
        s = (a[1][1] * p[0] - a[1][0] * p[1]) * idet
        t = (a[0][0] * p[1] - a[1][0] * p[0]) * idet
        s2 = (a[1][1] * a[2][0] - a[1][0] * a[2][1]) * idet
        t2 = (a[0][0] * a[2][1] - a[1][0] * a[2][0]) * idet
        s3 = (a[1][1] * a[3][0] - a[1][0] * a[3][1]) * idet
        t3 = (a[0][0] * a[3][1] - a[1][0] * a[3][0]) * idet
        a22 = a[2][2] - (a[2][0] * s2 + a[2][1] * t2)
        a32 = a[3][2] - (a[3][0] * s2 + a[3][1] * t2)
        a33 = a[3][3] - (a[3][0] * s3 + a[3][1] * t3)
        p2 = p[2] - (a[2][0] * s + a[2][1] * t)
        p3 = p[3] - (a[3][0] * s + a[3][1] * t)
        idet = 1.0 / (a22 * a33 - a32 * a32)
        u = (a33 * p2 - a32 * p3) * idet
        v = (a22 * p3 - a32 * p2) * idet
        s = s - (s2 * u + s3 * v)
        t = t - (t2 * u + t3 * v)
        for g in range(g0, 4):
            c = [cols[k][g - g0] for k in range(4)]
            new = rows[g] - ((c[0] * s + c[1] * t) + (c[2] * u + c[3] * v))
            if g == g0:
                p1 = p[1] - a[1][0] / a[0][0] * p[0]
                p3 = p3 - a32 / a22 * p2
                new = jnp.where(sub < r + 4, rows[g], new)
                new = jnp.where(sub == r + 1, p1, new)
                new = jnp.where(sub == r + 2, p2, new)
                new = jnp.where(sub == r + 3, p3, new)
            rows[g] = new
    inverse = []
    diag = jnp.zeros((8, 128), F32)
    for g in range(4):
        mask = lane == sub + (8 * g + 64)
        d = jnp.sum(jnp.where(mask, rows[g], 0.0), axis=1, keepdims=True)
        root = bc(jnp.sqrt(d))
        inverse.append(rows[g] / root)
        diag = diag + jnp.where(mask, root, 0.0)
    return jnp.concatenate(inverse, axis=0)[:, 0:32], jnp.sum(diag, axis=0, keepdims=True)[:, 64:96]


def kernel(
    days, r_ref, seed_ref, load_ref, str_ref,
    rb, rv, sv, pbuf, pc, abuf, r1, bbuf, r2, ybuf, ag, gbuf, fin, ga,
    local, send, recv,
):
    gr = lax.axis_index("gr")
    gc = lax.axis_index("gc")
    core = gr % 2
    x = gr // 4
    y = (gr // 2) % 2 * 2 + gc % 2
    z = gc // 2

    def dev(x, y, z, core):
        return ((x * 2 + y // 2) * 2 + core, z * 2 + y % 2)

    partner = dev(x, y, z, 1 - core)
    order = (1, 0, 2)
    xp = [dev((x + o) % 4, y, z, core) for o in (1, 2, 3)]
    yp = [dev(x, (y + o) % 4, z, core) for o in (1, 2, 3)]
    zp = [dev(x, y, (z + o) % 4, core) for o in (1, 2, 3)]
    plane = [dev((x + k // 4) % 4, y, (z + k % 4) % 4, core) for k in range(1, 16)]

    barrier = pltpu.get_barrier_semaphore()
    everyone = [partner] + xp + yp + zp
    for device in everyone:
        pl.semaphore_signal(barrier, inc=1, device_id=device, device_id_type=MESH)

    mine = pl.ds(pl.multiple_of(core * 128, 128), 128)
    loads = []
    for s in range(8):
        here = pl.ds(s * 1024, 1024)
        loads.append(
            (
                pltpu.make_async_copy(seed_ref.at[:, here], sv.at[:, here], local.at[s]),
                pltpu.make_async_copy(r_ref.at[:, here], rv.at[:, here], local.at[8 + s]),
            )
        )
        for copy in loads[s]:
            copy.start()
    spots = [(2 * q, 0, 512, q * 512) for q in range(4)]
    spots += [(2 * q + 1, j * 128, 128, 2048 + j * 512 + q * 128) for q in range(4) for j in range(4)]

    def columns(slab, offset, width, side):
        return r_ref.at[:, pl.ds(pl.multiple_of((slab * 2 + side) * 512 + offset, 128), width)]

    for slab, offset, width, spot in spots:
        here = rb.at[mine, pl.ds(spot, width)]
        pltpu.make_async_copy(columns(slab, offset, width, core), here, local.at[16]).start()
    halves = pltpu.make_async_copy(r_ref.at[:, 0:4096], rb.at[mine], local.at[16])

    pl.semaphore_wait(barrier, len(everyone))

    count = [0]
    pending = []

    def group(region, parts):
        k = count[0]
        count[0] += 1
        for src, dst, device in parts:
            pltpu.make_async_remote_copy(
                src_ref=src, dst_ref=dst, send_sem=send.at[k], recv_sem=recv.at[k],
                device_id=device, device_id_type=MESH,
            ).start()
        whole = pltpu.make_async_remote_copy(
            src_ref=region, dst_ref=region, send_sem=send.at[k], recv_sem=recv.at[k],
            device_id=partner, device_id_type=MESH,
        )
        pending.append(whole)
        return whole

    def single(ref, device):
        return group(ref, [(ref, ref, device)])

    swaps = group(
        rb.at[0:128],
        [
            (columns(slab, offset, width, 1 - core), rb.at[mine, pl.ds(spot, width)], partner)
            for slab, offset, width, spot in spots
        ],
    )

    rows = [slice(32 * c, 32 * c + 32) for c in range(2)]
    pieces = [slice(96 * c, 96 * c + 96) for c in range(2)]
    peers = ((xp, zp), (zp, xp))
    place = ((x, z), (z, x))
    swap_p = [None, None]

    first = None
    for s in range(8):
        here = slice(s * 1024, (s + 1) * 1024)
        for copy in loads[s]:
            copy.wait()
        part = sv[:, here].astype(F32)
        hi = part.astype(BF16)
        part = jnp.concatenate([hi, (part - hi.astype(F32)).astype(BF16)], axis=0)
        part = dot(part, rv[:, here], NT)
        first = part if first is None else first + part
    first = (first[0:64] + first[64:128]) / 1000.0
    pbuf[0, core, :, 0:128] = first
    swap_p[0] = single(pbuf.at[0, core, :, 0:128], partner)
    halves.wait()
    swap_p[0].wait_recv()
    first = jnp.concatenate([pbuf[0, 0, :, 0:128], pbuf[0, 1, :, 0:128]], axis=1)
    swaps.wait_recv()

    def part(h, p):
        return pl.ds(pl.multiple_of(h * 2048 + p * 512, 512), 512)

    def product(it, c):
        if it > 0:
            swap_p[c].wait_recv()
            p3 = split3((pbuf[it, 0, rows[c]] + pbuf[it, 1, rows[c]]) * (1.0 / days))
        else:
            p3 = split3(first[rows[c]] * (1.0 / days))
        moving = []
        for o in order + (3,):
            for h in range(2):
                to = (place[h][0] + o + 1) % 4
                out = fold(dot(p3, rb[:, part(h, to)]))
                for j in range(4):
                    abuf[it, c, h, to, j] = out[:, j * 128 : (j + 1) * 128]
            if o < 3:
                parts = []
                for h in range(2):
                    to = (place[h][0] + o + 1) % 4
                    parts.append((abuf.at[it, c, h, to], r1.at[it, c, h, o], peers[h][0][o]))
                moving.append(group(r1.at[it, c, 0, 0:2], parts))
        return moving

    def second(it, c, moving):
        for copy in moving:
            copy.wait_recv()
        parts = []
        for h in range(2):
            bbuf[it, c, h] = (abuf[it, c, h, place[h][0]] + r1[it, c, h, 0]) + (r1[it, c, h, 1] + r1[it, c, h, 2])
            for o in order:
                to = (place[h][1] + o + 1) % 4
                parts.append((bbuf.at[it, c, h, to], r2.at[it, c, h, o], peers[h][1][o]))
        return group(r2.at[it, c], parts)

    def third(it, c, moving):
        moving.wait_recv()
        for h in range(2):
            ybuf[it, c, y, h] = (bbuf[it, c, h, place[h][1]] + r2[it, c, h, 0]) + (r2[it, c, h, 1] + r2[it, c, h, 2])
        here = ybuf.at[it, c, y]
        return group(ybuf.at[it, c, 0:3], [(here, here, yp[o]) for o in order])

    def reduced(it, c, moving):
        moving.wait_recv()
        return jnp.concatenate(
            [(ybuf[it, c, 0, h] + ybuf[it, c, 1, h]) + (ybuf[it, c, 2, h] + ybuf[it, c, 3, h]) for h in range(2)],
            axis=1,
        )

    def gather1(it, c, done):
        parts = []
        for h in range(2):
            ag[it, c, h, place[h][0], place[h][1]] = done[:, 128 * h : 128 * h + 128]
        for h in range(2):
            block = ag.at[it, c, h, place[h][0], place[h][1]]
            parts += [(block, block, peers[h][1][o]) for o in order]
        return group(r2.at[it, c], parts)

    def gather2(it, c, moving):
        moving.wait_recv()
        sent = []
        for o in order:
            parts = []
            for h in range(2):
                block = ag.at[it, c, h, place[h][0]]
                parts.append((block, block, peers[h][0][o]))
            sent.append(group(r1.at[it, c, 0, 0:2], parts))
        return sent, project(it, c, 3)

    def project(it, c, o):
        total = None
        for h in range(2):
            p = (place[h][0] + 3 - o) % 4
            piece = split3(jnp.concatenate([ag[it, c, h, p, j] for j in range(4)], axis=1))
            pc[pieces[c], part(h, p)] = piece
            term = dot(piece, rb[:, part(h, p)], NT)
            total = term if total is None else total + term
        return total

    def projected(it, c, sent, total):
        for o, copy in zip(order, sent):
            copy.wait_recv()
            total = total + project(it, c, o)
        pbuf[it + 1, core, rows[c]] = fold(total)
        swap_p[c] = single(pbuf.at[it + 1, core, rows[c]], partner)

    def squares(it, c):
        for k in range(c + 1):
            square = dot(pc[pieces[c]], pc[pieces[k]], NT)
            gbuf[it, core, c, :, 32 * k : 32 * k + 32] = fold2(square)
        swap_g[c] = single(gbuf.at[it, core, c], partner)

    swap_g = [None, None]
    moving = [product(0, c) for c in range(2)]
    for it in range(ITERS):
        if it > 0:
            swap_g[0].wait_recv()
            la, da = factor32(gbuf[it - 1, 0, 0, :, 0:32] + gbuf[it - 1, 1, 0, :, 0:32])
        moving[0] = second(it, 0, moving[0])
        if it > 0:
            swap_g[1].wait_recv()
            low = gbuf[it - 1, 0, 1, :, 0:64] + gbuf[it - 1, 1, 1, :, 0:64]
            lba, lb, db = lower(low, la)
            str_ref[it - 1 : it, :] = jnp.concatenate([da, db], axis=1)
        moving[1] = second(it, 1, moving[1])
        moving = [third(it, c, moving[c]) for c in range(2)]
        if it == ITERS - 1:
            break
        for c in range(2):
            done = raw = reduced(it, c, moving[c])
            if it > 0:
                done = exact(la, raw) if c == 0 else exact(lba, above) + exact(lb, raw)
            above = raw
            moving[c] = gather1(it, c, done)
        moving = [gather2(it, c, moving[c]) for c in range(2)]
        for c in range(2):
            projected(it, c, *moving[c])
        moving = [product(it + 1, c) for c in range(2)]
        for c in range(2):
            squares(it, c)

    it = ITERS - 1
    spot = x * 4 + z
    slabs, grams, wide = [], [], []
    for c in range(2):
        raw = reduced(it, c, moving[c])
        done = exact(la, raw) if c == 0 else exact(lba, above) + exact(lb, raw)
        above = raw
        wide.append(split3(done))
        gram = jnp.concatenate([fold2(dot(wide[c], wide[k], NT)) for k in range(c + 1)], axis=1)
        size = 8 * (c + 1)
        ga[c, spot, 0:size] = jnp.concatenate([gram[k : k + size] for k in range(0, 32, size)], axis=1)
        here = ga.at[c, spot, 0:size]
        grams.append(group(ga.at[c, 0:15, 0:size], [(here, here, device) for device in plane]))
        fin[z, rows[c]] = jnp.where(y < 2, done[:, 0:128], done[:, 128:256])
        here = fin.at[z, rows[c]]
        slabs.append(group(fin.at[0:3, rows[c]], [(here, here, zp[o]) for o in order]))
    for c in range(2):
        size = 8 * (c + 1)
        grams[c].wait_recv()
        total = [ga[c, k, 0:size] + ga[c, k + 1, 0:size] for k in range(0, 16, 2)]
        while len(total) > 1:
            total = [total[k] + total[k + 1] for k in range(0, len(total), 2)]
        gbuf[it, core, c, 0:size] = total[0]
        swap_g[c] = single(gbuf.at[it, core, c, 0:size], partner)
        if c == 0:
            swap_g[0].wait_recv()
            gram = gbuf[it, 0, 0, 0:8] + gbuf[it, 1, 0, 0:8]
            la, da = factor32(jnp.concatenate([gram[:, k : k + 32] for k in range(0, 128, 32)], axis=0))
    swap_g[1].wait_recv()
    gram = gbuf[it, 0, 1, 0:16] + gbuf[it, 1, 1, 0:16]
    lba, lb, db = lower(jnp.concatenate([gram[:, 0:64], gram[:, 64:128]], axis=0), la)
    str_ref[it : it + 1, :] = jnp.concatenate([da, db], axis=1)
    for copy in slabs:
        copy.wait_recv()
    slab = jnp.concatenate([fin[k] for k in range(4)], axis=1)
    scale = math.sqrt(8192)
    load_ref[0:32] = exact(la, slab[0:32]) * scale
    load_ref[32:64] = (exact(lba, slab[0:32]) + exact(lb, slab[32:64])) * scale
    for copy in pending:
        copy.wait_send()


def lower(gram, la):
    b = exact(gram[:, 0:32], la, NT)
    lb, db = factor32(gram[:, 32:64] - exact(b, b, NT))
    return -exact(exact(lb, b), la), lb, db


SEMS = 80


def local(days, returns, start_seed):
    seed = start_seed.T
    vm = pltpu.VMEM
    out = pl.pallas_call(
        functools.partial(kernel, days),
        out_shape=(
            jax.ShapeDtypeStruct((64, 512), F32),
            jax.ShapeDtypeStruct((3, 64), F32),
        ),
        in_specs=[pl.BlockSpec(memory_space=pltpu.HBM)] * 2,
        out_specs=[pl.BlockSpec(memory_space=pltpu.VMEM)] * 2,
        scratch_shapes=[
            vm((256, 4096), BF16),
            vm((128, 8192), BF16),
            vm((64, 8192), jnp.int32),
            vm((3, 2, 64, 256), F32),
            vm((192, 4096), BF16),
            vm((3, 2, 2, 4, 4, 32, 128), F32),
            vm((3, 2, 2, 3, 4, 32, 128), F32),
            vm((3, 2, 2, 4, 32, 128), F32),
            vm((3, 2, 2, 3, 32, 128), F32),
            vm((3, 2, 4, 2, 32, 128), F32),
            vm((2, 2, 2, 4, 4, 32, 128), F32),
            vm((3, 2, 2, 32, 128), F32),
            vm((4, 64, 128), F32),
            vm((2, 16, 16, 128), F32),
            pltpu.SemaphoreType.DMA((17,)),
            pltpu.SemaphoreType.DMA((SEMS,)),
            pltpu.SemaphoreType.DMA((SEMS,)),
        ],
        compiler_params=pltpu.CompilerParams(
            collective_id=0, has_side_effects=True, vmem_limit_bytes=67043328
        ),
        name="power",
    )(returns, seed)
    return out[0].T, out[1]


def solution(mesh):
    placed = (P(("gr", "gc"), None), P())
    return jax.shard_map(
        functools.partial(local, 16384), mesh=mesh, in_specs=placed,
        out_specs=(P("gr", None), P()), check_vma=False,
    )
```

time: 546 us -> 93 us (0.17)
  waiting for transfers between devices: 452 us -> 0 us
  Pallas kernels: 0 us -> 89.4 us
  matrix products: 38.2 us -> 0 us
  other arithmetic: 37.7 us -> 0 us
  between operations: 13.9 us -> 0.64 us
    psum x3 -> x0, waiting for transfers between devices: 451 us -> none  [local(): applied = lax.psum(partial_apply, ('gr', 'gc')) / day_count]
    pallas_call x0 -> x1, Pallas kernels: none -> 89.4 us  [local(): pl.pallas_call(functools.partial(kernel, days), out_shape=(jax.ShapeDtype...]
    another operation x16 -> x0, other arithmetic: 36.9 us -> none  [the longest x9 19.6 us: orthonormal(): factor = jnp.linalg.cholesky(inner_gram)]
    dot_general x9 -> x0, matrix products: 27.8 us -> none  [the longest x3 12.4 us: local_gram(): return jnp.dot(applied.T, applied, precision=lax.Precision.HIGHEST)]
    another operation x3 -> x0, matrix products: 10.4 us -> none  [orthonormal(): lax.linalg.triangular_solve(factor, applied, left_side=False, lower=True,...]
  transfers between devices with their start and end apart: 3 -> 0, of which waited for: 3 -> 0; matrix products, arithmetic and copies ran while one was open for 0% -> 0% of each run, Pallas kernels for 0% -> 0%
where the time goes in v2:
time: 93 us; the launch traced here: 92.8 us
  Pallas kernels  89.4 us (96%)
  local copies, waits for them, and re-layouts  2.83 us (3%)
    pallas_call x1, Pallas kernels, local(): pl.pallas_call(functools.partial(kernel, days), out_shape=(jax.ShapeDtype...  89.4 us
    unnamed x2, local copies, waits for them, and re-layouts  2.83 us

profile of v2, /device:TPU:1, one launch (start us, length us, event | category | flops | bytes accessed | tf_op | source)
XLA Modules:
  0.0 92.8 jit_solution(3965002139937224983)
XLA Ops:
  0.6 89.4 %power.1 = (f32[64,512]{1,0:T(8,128)}, f32[3,64]{1,0:T(4,128)}) custom-call(bf16[128,8192]{1,0:T(8,128)(2,1)} %r_ref.1, s32[64,8192]{1,0:T(8,128)} %bitcast.2), custom_call_target="tpu_custom_call" | custom-call | tf_op jit(solution)/shard_map/power/pallas_call | solution.py:376
  90.0 1.6 %copy.6 = f32[512,64]{0,1:T(8,128)} copy(f32[512,64]{0,1:T(8,128)} %bitcast.3) | data formatting | bytes 262144
  91.6 1.3 %copy.7 = f32[3,64]{1,0:T(4,128)} copy(f32[3,64]{1,0:T(4,128)} %get-tuple-element.9) | data formatting | bytes 1536

commit v3 on v2

--- a/solution.py
+++ b/solution.py
@@ -163,6 +163,10 @@
         pending.append(whole)
         return whole
 
+    def finish():
+        while pending:
+            pending.pop().wait_send()
+
     def single(ref, device):
         return group(ref, [(ref, ref, device)])
 
@@ -176,8 +180,19 @@
 
     rows = [slice(32 * c, 32 * c + 32) for c in range(2)]
     pieces = [slice(96 * c, 96 * c + 96) for c in range(2)]
-    peers = ((xp, zp), (zp, xp))
-    place = ((x, z), (z, x))
+    def either(a, b):
+        return core * a + (1 - core) * b
+
+    def mix(a, b):
+        return either(a[0], b[0]), [tuple(either(m, n) for m, n in zip(i, j)) for i, j in zip(a[1], b[1])]
+
+    ax, ay, az = (x, xp), (y, yp), (z, zp)
+    streams = (
+        (((ax, az, ay), (az, ay, ax)), ((ay, ax, az), (mix(az, ax), mix(ax, az), ay))),
+        (((ax, az, ay), (az, ax, ay)), ((ax, az, ay), (az, ax, ay))),
+    )
+    place = [[[[d[0] for d in h] for h in c] for c in r] for r in streams]
+    peers = [[[[d[1] for d in h] for h in c] for c in r] for r in streams]
     swap_p = [None, None]
 
     first = None
@@ -208,18 +223,24 @@
         else:
             p3 = split3(first[rows[c]] * (1.0 / days))
         moving = []
+
+        def go(o):
+            parts = []
+            for h in range(2):
+                to = (place[it > 0][c][h][0] + o + 1) % 4
+                parts.append((abuf.at[it, c, h, to], r1.at[it, c, h, o], peers[it > 0][c][h][0][o]))
+            return parts
+
         for o in order + (3,):
             for h in range(2):
-                to = (place[h][0] + o + 1) % 4
+                to = (place[it > 0][c][h][0] + o + 1) % 4
                 out = fold(dot(p3, rb[:, part(h, to)]))
                 for j in range(4):
                     abuf[it, c, h, to, j] = out[:, j * 128 : (j + 1) * 128]
-            if o < 3:
-                parts = []
-                for h in range(2):
-                    to = (place[h][0] + o + 1) % 4
-                    parts.append((abuf.at[it, c, h, to], r1.at[it, c, h, o], peers[h][0][o]))
-                moving.append(group(r1.at[it, c, 0, 0:2], parts))
+            if o == 0:
+                moving.append(group(r1.at[it, c, :, 0:2], go(1) + go(0)))
+            elif o == 2:
+                moving.append(group(r1.at[it, c, 0, 0:2], go(2)))
         return moving
 
     def second(it, c, moving):
@@ -227,18 +248,21 @@
             copy.wait_recv()
         parts = []
         for h in range(2):
-            bbuf[it, c, h] = (abuf[it, c, h, place[h][0]] + r1[it, c, h, 0]) + (r1[it, c, h, 1] + r1[it, c, h, 2])
+            bbuf[it, c, h] = (abuf[it, c, h, place[it > 0][c][h][0]] + r1[it, c, h, 0]) + (r1[it, c, h, 1] + r1[it, c, h, 2])
             for o in order:
-                to = (place[h][1] + o + 1) % 4
-                parts.append((bbuf.at[it, c, h, to], r2.at[it, c, h, o], peers[h][1][o]))
+                to = (place[it > 0][c][h][1] + o + 1) % 4
+                parts.append((bbuf.at[it, c, h, to], r2.at[it, c, h, o], peers[it > 0][c][h][1][o]))
         return group(r2.at[it, c], parts)
 
     def third(it, c, moving):
         moving.wait_recv()
         for h in range(2):
-            ybuf[it, c, y, h] = (bbuf[it, c, h, place[h][1]] + r2[it, c, h, 0]) + (r2[it, c, h, 1] + r2[it, c, h, 2])
-        here = ybuf.at[it, c, y]
-        return group(ybuf.at[it, c, 0:3], [(here, here, yp[o]) for o in order])
+            ybuf[it, c, place[it > 0][c][h][2], h] = (bbuf[it, c, h, place[it > 0][c][h][1]] + r2[it, c, h, 0]) + (r2[it, c, h, 1] + r2[it, c, h, 2])
+        parts = []
+        for h in range(2):
+            here = ybuf.at[it, c, place[it > 0][c][h][2], h]
+            parts += [(here, here, peers[it > 0][c][h][2][o]) for o in order]
+        return group(ybuf.at[it, c, 0:3], parts)
 
     def reduced(it, c, moving):
         moving.wait_recv()
@@ -250,27 +274,33 @@
     def gather1(it, c, done):
         parts = []
         for h in range(2):
-            ag[it, c, h, place[h][0], place[h][1]] = done[:, 128 * h : 128 * h + 128]
-        for h in range(2):
-            block = ag.at[it, c, h, place[h][0], place[h][1]]
-            parts += [(block, block, peers[h][1][o]) for o in order]
-        return group(r2.at[it, c], parts)
+            ag[it, c, h, place[it > 0][c][h][0], place[it > 0][c][h][1]] = done[:, 128 * h : 128 * h + 128]
+        for h in range(2):
+            block = ag.at[it, c, h, place[it > 0][c][h][0], place[it > 0][c][h][1]]
+            parts += [(block, block, peers[it > 0][c][h][1][o]) for o in order]
+        near = group(r2.at[it, c], parts)
+        parts = []
+        for h in range(2):
+            block = ag.at[it, c, h, place[it > 0][c][h][0], place[it > 0][c][h][1]]
+            parts += [(block, block, peers[it > 0][c][h][0][o]) for o in order]
+        return near, group(r2.at[it, c], parts)
 
     def gather2(it, c, moving):
-        moving.wait_recv()
-        sent = []
+        moving[0].wait_recv()
+        sent = [moving[1]]
         for o in order:
             parts = []
             for h in range(2):
-                block = ag.at[it, c, h, place[h][0]]
-                parts.append((block, block, peers[h][0][o]))
-            sent.append(group(r1.at[it, c, 0, 0:2], parts))
+                for k in (1, 2, 3):
+                    block = ag.at[it, c, h, place[it > 0][c][h][0], (place[it > 0][c][h][1] + k) % 4]
+                    parts.append((block, block, peers[it > 0][c][h][0][o]))
+            sent.append(group(r2.at[it, c], parts))
         return sent, project(it, c, 3)
 
     def project(it, c, o):
         total = None
         for h in range(2):
-            p = (place[h][0] + 3 - o) % 4
+            p = (place[it > 0][c][h][0] + 3 - o) % 4
             piece = split3(jnp.concatenate([ag[it, c, h, p, j] for j in range(4)], axis=1))
             pc[pieces[c], part(h, p)] = piece
             term = dot(piece, rb[:, part(h, p)], NT)
@@ -278,7 +308,8 @@
         return total
 
     def projected(it, c, sent, total):
-        for o, copy in zip(order, sent):
+        sent[0].wait_recv()
+        for o, copy in zip(order, sent[1:]):
             copy.wait_recv()
             total = total + project(it, c, o)
         pbuf[it + 1, core, rows[c]] = fold(total)
@@ -291,18 +322,19 @@
         swap_g[c] = single(gbuf.at[it, core, c], partner)
 
     swap_g = [None, None]
-    moving = [product(0, c) for c in range(2)]
+    moving = [product(0, 0)]
+    moving.append(product(0, 1))
     for it in range(ITERS):
         if it > 0:
             swap_g[0].wait_recv()
             la, da = factor32(gbuf[it - 1, 0, 0, :, 0:32] + gbuf[it - 1, 1, 0, :, 0:32])
         moving[0] = second(it, 0, moving[0])
+        moving[1] = second(it, 1, moving[1])
         if it > 0:
             swap_g[1].wait_recv()
             low = gbuf[it - 1, 0, 1, :, 0:64] + gbuf[it - 1, 1, 1, :, 0:64]
             lba, lb, db = lower(low, la)
             str_ref[it - 1 : it, :] = jnp.concatenate([da, db], axis=1)
-        moving[1] = second(it, 1, moving[1])
         moving = [third(it, c, moving[c]) for c in range(2)]
         if it == ITERS - 1:
             break
@@ -313,11 +345,13 @@
             above = raw
             moving[c] = gather1(it, c, done)
         moving = [gather2(it, c, moving[c]) for c in range(2)]
-        for c in range(2):
-            projected(it, c, *moving[c])
-        moving = [product(it + 1, c) for c in range(2)]
-        for c in range(2):
-            squares(it, c)
+        projected(it, 0, *moving[0])
+        late = moving[1]
+        moving = [product(it + 1, 0)]
+        projected(it, 1, *late)
+        moving.append(product(it + 1, 1))
+        squares(it, 0)
+        squares(it, 1)
 
     it = ITERS - 1
     spot = x * 4 + z
@@ -347,18 +381,22 @@
             swap_g[0].wait_recv()
             gram = gbuf[it, 0, 0, 0:8] + gbuf[it, 1, 0, 0:8]
             la, da = factor32(jnp.concatenate([gram[:, k : k + 32] for k in range(0, 128, 32)], axis=0))
+            for copy in slabs:
+                copy.wait_recv()
+            slab = jnp.concatenate([fin[k] for k in range(4)], axis=1)
+            upper = exact(la, slab[0:32])
+            scale = math.sqrt(8192)
+            load_ref[0:32] = upper * scale
+            finish()
     swap_g[1].wait_recv()
     gram = gbuf[it, 0, 1, 0:16] + gbuf[it, 1, 1, 0:16]
-    lba, lb, db = lower(jnp.concatenate([gram[:, 0:64], gram[:, 64:128]], axis=0), la)
+    gram = jnp.concatenate([gram[:, 0:64], gram[:, 64:128]], axis=0)
+    cross = exact(gram[:, 0:32], la, NT)
+    rest = slab[32:64] - exact(cross, upper)
+    lb, db = factor32(gram[:, 32:64] - exact(cross, cross, NT))
+    load_ref[32:64] = exact(lb, rest) * scale
     str_ref[it : it + 1, :] = jnp.concatenate([da, db], axis=1)
-    for copy in slabs:
-        copy.wait_recv()
-    slab = jnp.concatenate([fin[k] for k in range(4)], axis=1)
-    scale = math.sqrt(8192)
-    load_ref[0:32] = exact(la, slab[0:32]) * scale
-    load_ref[32:64] = (exact(lba, slab[0:32]) + exact(lb, slab[32:64])) * scale
-    for copy in pending:
-        copy.wait_send()
+    finish()
 
 
 def lower(gram, la):
@@ -367,7 +405,7 @@
     return -exact(exact(lb, b), la), lb, db
 
 
-SEMS = 80
+SEMS = 60
 
 
 def local(days, returns, start_seed):

time: 93 us -> 89.7 us (0.965)
  Pallas kernels: 89.4 us -> 86.1 us
    pallas_call x1, Pallas kernels: 89.4 us -> 86.1 us  [local(): pl.pallas_call(functools.partial(kernel, days), out_shape=(jax.ShapeDtype...]
where the time goes in v3:
time: 89.7 us; the launch traced here: 89.6 us
  Pallas kernels  86.1 us (96%)
  local copies, waits for them, and re-layouts  2.83 us (3%)
    pallas_call x1, Pallas kernels, local(): pl.pallas_call(functools.partial(kernel, days), out_shape=(jax.ShapeDtype...  86.1 us
    unnamed x2, local copies, waits for them, and re-layouts  2.83 us

profile of v3, /device:TPU:1, one launch (start us, length us, event | category | flops | bytes accessed | tf_op | source)
XLA Modules:
  0.0 89.6 jit_solution(8103319936343752247)
XLA Ops:
  0.6 86.1 %power.1 = (f32[64,512]{1,0:T(8,128)}, f32[3,64]{1,0:T(4,128)}) custom-call(bf16[128,8192]{1,0:T(8,128)(2,1)} %r_ref.1, s32[64,8192]{1,0:T(8,128)} %bitcast.2), custom_call_target="tpu_custom_call" | custom-call | tf_op jit(solution)/shard_map/power/pallas_call | solution.py:414
  86.8 1.6 %copy.6 = f32[512,64]{0,1:T(8,128)} copy(f32[512,64]{0,1:T(8,128)} %bitcast.3) | data formatting | bytes 262144
  88.3 1.3 %copy.7 = f32[3,64]{1,0:T(4,128)} copy(f32[3,64]{1,0:T(4,128)} %get-tuple-element.9) | data formatting | bytes 1536
